TPU v7x, 32 devices: a whole 2x2x4 slice. The times are simulated.
32 devices in a mesh: grp: 2 (over y), trade: 4 (over z), date: 2 (over x), path: 2 (over core).
Axes of the slice: x: 2, y: 2, z: 4, core: 2. Of those that a mesh axis runs over, the one named last changes fastest.
Arguments:
- driver_increments: float32 [16, 256, 128], P(('grp', 'date'), 'path'), parts along dimension 0, may hold values from -4 to 4
- persistence_ratio: float32 [16, 128], P(('grp', 'date')), parts along dimension 0, may hold values from 0 to 1, as said below
- deal_sensitivity: bfloat16 [128, 65536], P(None, ('grp', 'trade')), parts along dimension 1, may hold values from -0.5 to 0.5
- signed_notional: float32 [65536], P(('grp', 'trade')), parts along dimension 0, may hold values from -0.4 to 0.4
- batch_obligor: int32 [512], P(('grp', 'trade')), parts along dimension 0, may hold values from 0 to 127, as said below
- collateral_ceiling: float32 [256], P(('grp', 'trade')), parts along dimension 0, may hold values from -1 to 1
- default_discount_mass: float32 [16, 128], P(('grp', 'date'), 'trade'), parts along dimension 0, may hold values from 0.1 to 1
Outputs:
- exposure_profile: float32 [16, 128], P(('grp', 'date'), 'trade'), parts along dimension 0
- shock_gradient: float32 [16, 256, 128], P(('grp', 'date'), 'path'), parts along dimension 0
There are 2 independent parts, one for each index of `grp`. A program takes and returns all parts, laid end to end along the dimension named above; each array names one. Nothing has to cross between parts.
Inputs may be any that keep to these rules, and one draw needn't show every extreme that they name: `persistence_ratio`: strictly between 0 and 1. `batch_obligor`: counterparty c belongs to trade shard c // 32. Of the 64 trade blocks of one trade shard, at most 32 have counterparties on any one trade shard, and in every trade shard some counterparty shard receives exactly 32 of them.
All inputs are finite; a program needn't handle non-finite values.
Results may differ from a plain program's by a relative error of at most 0.0019.
Values sent between devices are 32-bit elements; how exact they have to be, the bound alone decides.
No kernel may reach another device: no remote copies, remote signals or barrier semaphores. Data moves between devices by JAX's collectives and lax.ppermute only.
A program may use at most 64 MiB of HBM per device.

v0:
```python
import jax
import jax.numpy as jnp
from jax import lax
from jax.sharding import PartitionSpec as P

block_width = 128
cluster_extent = 512
highest = lax.Precision.HIGHEST


def entering(value, axis, combine, identity, reverse):
    length, index = (lax.axis_size(axis), lax.axis_index(axis))
    everything = jax.tree.map(lambda part: lax.all_gather(part, axis), value)
    start = jax.tree.map(
        lambda part, zero: jnp.broadcast_to(jnp.asarray(zero, part.dtype), part.shape),
        value,
        identity,
    )

    def hop(k, before):
        at = length - 1 - k if reverse else k
        reached = at > index if reverse else at < index
        new = combine(before, jax.tree.map(lambda part: part[at], everything))
        return jax.tree.map(lambda a, b: jnp.where(reached, a, b), new, before)

    return lax.fori_loop(0, length, hop, start)


def compose(earlier, later):
    return (later[0] * earlier[0], later[0] * earlier[1] + later[1])


def reverse_chain(direct, persistence_ratio):
    date_count = direct.shape[0]
    factor_gain = jnp.ones((direct.shape[2],), jnp.float32)
    message = jnp.zeros(direct.shape[1:], jnp.float32)
    for date_step in reversed(range(date_count)):
        message = persistence_ratio[date_step][None, :] * (direct[date_step] + message)
        factor_gain = persistence_ratio[date_step] * factor_gain
    identity = (jnp.ones_like(factor_gain), jnp.zeros_like(message))
    _, arriving = entering((factor_gain, message), "date", compose, identity, True)
    adjoints = []
    message = arriving
    for date_step in reversed(range(date_count)):
        adjoint = direct[date_step] + message
        adjoints.append(adjoint)
        message = persistence_ratio[date_step][None, :] * adjoint
    return jnp.stack(adjoints[::-1])


def shards(
    driver_increments,
    persistence_ratio,
    deal_sensitivity,
    signed_notional,
    batch_obligor,
    collateral_ceiling,
    default_discount_mass,
):
    date_count, path_count, factor_count = driver_increments.shape
    factor_gain = jnp.ones((factor_count,), jnp.float32)
    carried = jnp.zeros((path_count, factor_count), jnp.float32)
    for date_step in range(date_count):
        carried = persistence_ratio[date_step][None, :] * carried + driver_increments[date_step]
        factor_gain = persistence_ratio[date_step] * factor_gain
    identity = (jnp.ones_like(factor_gain), jnp.zeros_like(carried))
    _, arriving = entering((factor_gain, carried), "date", compose, identity, False)
    states = []
    carried = arriving
    for date_step in range(date_count):
        carried = persistence_ratio[date_step][None, :] * carried + driver_increments[date_step]
        states.append(carried)
    row_count = date_count * path_count
    state_bf = jnp.stack(states).reshape(row_count, factor_count).astype(jnp.bfloat16)
    deal_ordinal = deal_sensitivity.shape[1]
    block_count = deal_ordinal // block_width
    cluster_ordinal = deal_ordinal // cluster_extent
    per_group = cluster_extent // block_width

    def value_group(group_index, block_sums):
        opening_offset = group_index * cluster_extent
        sensitivity_portion = lax.dynamic_slice_in_dim(
            deal_sensitivity, opening_offset, cluster_extent, 1
        )
        size_part = lax.dynamic_slice_in_dim(signed_notional, opening_offset, cluster_extent, 0)
        linear = jnp.dot(state_bf, sensitivity_portion, preferred_element_type=jnp.float32)
        trade_value = jax.nn.softplus(linear) * size_part[None, :]
        summed = trade_value.reshape(row_count, per_group, block_width).sum(axis=2)
        return lax.dynamic_update_slice_in_dim(block_sums, summed.T, group_index * per_group, 0)

    block_sums = lax.fori_loop(
        0, cluster_ordinal, value_group, jnp.zeros((block_count, row_count), jnp.float32)
    )
    cpty_dev = collateral_ceiling.shape[0]
    shard_count = lax.axis_size("trade")
    ownership = (
        batch_obligor[:, None] == jnp.arange(cpty_dev * shard_count, dtype=jnp.int32)[None, :]
    ).astype(jnp.float32)
    partial_value = lax.dot_general(
        ownership, block_sums, (((0,), (0,)), ((), ())), precision=highest
    )
    netted = lax.psum_scatter(partial_value, "trade", scatter_dimension=0, tiled=True)
    shifted = netted - collateral_ceiling[:, None]
    exposure = jax.nn.softplus(shifted).reshape(cpty_dev, date_count, path_count)
    path_total = lax.psum(jnp.sum(exposure, axis=2).T, "path")
    exposure_profile = path_total / (path_count * lax.axis_size("path"))
    net_adjoint = (
        default_discount_mass.T[:, :, None]
        * jax.nn.sigmoid(shifted).reshape(cpty_dev, date_count, path_count)
    ).reshape(cpty_dev, row_count)
    gathered = lax.all_gather(net_adjoint, "trade", axis=0, tiled=True)
    block_adjoint = jnp.dot(ownership, gathered, precision=highest)

    def pull_group(group_index, running):
        opening_offset = group_index * cluster_extent
        sensitivity_portion = lax.dynamic_slice_in_dim(
            deal_sensitivity, opening_offset, cluster_extent, 1
        )
        size_part = lax.dynamic_slice_in_dim(signed_notional, opening_offset, cluster_extent, 0)
        linear = jnp.dot(state_bf, sensitivity_portion, preferred_element_type=jnp.float32)
        slope_term = jax.nn.sigmoid(linear) * size_part[None, :]
        upstream = lax.dynamic_slice_in_dim(block_adjoint, group_index * per_group, per_group, 0)
        value_adjoint = (
            (upstream.T[:, :, None] * slope_term.reshape(row_count, per_group, block_width))
            .reshape(row_count, cluster_extent)
            .astype(jnp.bfloat16)
        )
        product = lax.dot_general(
            value_adjoint,
            sensitivity_portion,
            (((1,), (1,)), ((), ())),
            preferred_element_type=jnp.float32,
        )
        return running + product

    direct = lax.fori_loop(
        0, cluster_ordinal, pull_group, jnp.zeros((row_count, factor_count), jnp.float32)
    )
    direct = direct.reshape(date_count, path_count, factor_count)
    summed = lax.psum(direct, "trade")
    shock_gradient = reverse_chain(summed, persistence_ratio)
    return (exposure_profile, shock_gradient)


def solution(mesh):
    return jax.shard_map(
        shards,
        mesh=mesh,
        in_specs=(
            P(("grp", "date"), "path", None),
            P(("grp", "date"), None),
            P(None, ("grp", "trade")),
            P(("grp", "trade")),
            P(("grp", "trade")),
            P(("grp", "trade")),
            P(("grp", "date"), "trade"),
        ),
        out_specs=(P(("grp", "date"), "trade"), P(("grp", "date"), "path", None)),
        check_vma=False,
    )
```

profile of v0, /device:TPU:0, one launch (start us, length us, event | category | flops | bytes accessed | tf_op | source)
XLA Modules:
  0.0 200.2 jit_solution(7079904627721618631)
XLA Ops:
  8.8 5.1 %all-gather = f32[2,1,128]{2,1,0:T(1,128)S(1)} all-gather(f32[1,1,128]{2,1,0:T(1,128)S(1)} %get-tuple-element.550), channel_id=1, replica_groups=mesh['grp'=2,'trade'=4,'date'=2,'path'=2] {'date'}, dimensions={0}, use_global_device_ids=true | all-gather | bytes 1536 | tf_op jit(solution)/shard_map/all_gather | solution.py:13
  14.8 4.9 %all_gather.20 = f32[2,128,128]{2,1,0:T(8,128)S(1)} all-gather(f32[1,128,128]{2,1,0:T(8,128)S(1)} %multiply_add_fusion), channel_id=1, replica_groups=mesh['grp'=2,'trade'=4,'date'=2,'path'=2] {'date'}, dimensions={0}, use_global_device_ids=true | all-gather | bytes 196608 | tf_op jit(solution)/shard_map/all_gather | solution.py:13
  20.9 41.0 %while.57 = (s32[]{:T(128)}, f32[64,512]{1,0:T(8,128)S(1)}, bf16[128,8192]{1,0:T(8,128)(2,1)}, bf16[512,128]{1,0:T(8,128)(2,1)S(1)}, f32[8192]{0:T(1024)}, /*ind...) while((s32[]{:T(128)}, f32[64,512]{1,0:T(8,128)S(1)}, ...), condition=%wide.region_4.5_spmd, body=%wide.region_2.4_spmd.sunk | while | flops 69203976 | bytes 293085 | solution.py:91
  21.7 1.8 bitcast_reduce_fusion.2
  24.2 1.8 bitcast_reduce_fusion.2
  26.8 1.8 bitcast_reduce_fusion.2
  29.4 1.8 bitcast_reduce_fusion.2
  31.9 1.8 bitcast_reduce_fusion.2
  34.5 1.8 bitcast_reduce_fusion.2
  37.0 1.8 bitcast_reduce_fusion.2
  39.6 1.7 bitcast_reduce_fusion.2
  42.2 1.8 bitcast_reduce_fusion.2
  44.7 1.8 bitcast_reduce_fusion.2
  47.3 1.8 bitcast_reduce_fusion.2
  49.8 1.7 bitcast_reduce_fusion.2
  52.4 1.8 bitcast_reduce_fusion.2
  55.0 1.8 bitcast_reduce_fusion.2
  57.5 1.8 bitcast_reduce_fusion.2
  60.1 1.8 bitcast_reduce_fusion.2
  63.1 21.4 %reduce-scatter.2.cloned.1.call-done = f32[32,512]{1,0:T(8,128)} async-done(((f32[128,512]{1,0:T(8,128)}), f32[32,512]{1,0:T(8,128)}) %reduce-scatter.2.cloned.1.call-update) | async-done | bytes 65552 | tf_op jit(solution)/shard_map/reduce_scatter | solution.py:102
  85.6 13.8 %all_gather.21 = f32[128,512]{1,0:T(8,128)S(1)} all-gather(f32[32,512]{1,0:T(8,128)S(1)} %get-tuple-element.544), channel_id=1, replica_groups=mesh['grp'=2,'trade'=4,'date'=2,'path'=2] {'trade'}, dimensions={0}, use_global_device_ids=true | all-gather | bytes 327680 | tf_op jit(solution)/shard_map/all_gather | solution.py:111
  99.7 50.3 %while.59 = (s32[]{:T(128)}, f32[512,128]{1,0:T(8,128)S(1)}, f32[64,512]{1,0:T(8,128)S(1)}, bf16[128,8192]{1,0:T(8,128)(2,1)}, bf16[512,128]{1,0:T(8,128)(2,1)S(...) while((s32[]{:T(128)}, f32[512,128]{1,0:T(8,128)S(1)}, ...), condition=%wide.region_9.10_spmd.clone, body=%wide.region_8.9_spmd.clone.sunk | while | flops 135921680 | bytes 3063530 | solution.py:136
  101.3 1.6 fusion.50
  104.4 1.6 fusion.50
  113.8 1.6 fusion.50
  129.5 1.6 fusion.50
  132.7 1.6 fusion.50
  145.3 1.6 fusion.50
  150.8 4.2 %all-gather.1 = f32[2,1,128]{2,1,0:T(1,128)S(1)} all-gather(f32[1,1,128]{2,1,0:T(1,128)S(1)} %get-tuple-element.546), channel_id=1, replica_groups=mesh['grp'=2,'trade'=4,'date'=2,'path'=2] {'date'}, dimensions={0}, use_global_device_ids=true | all-gather | bytes 1536 | tf_op jit(solution)/shard_map/all_gather | solution.py:13
  155.1 3.4 %psum.14 = f32[4,32]{0,1:T(8,128)S(1)} all-reduce(f32[4,32]{0,1:T(8,128)S(1)} %bitcast.153), channel_id=1, replica_groups=mesh['grp'=2,'trade'=4,'date'=2,'path'=2] {'path'}, use_global_device_ids=true, to_apply=%region_7.8 | all-reduce | flops 128 | bytes 1024 | tf_op jit(solution)/shard_map/psum | solution.py:105
  159.1 25.7 %all-reduce.2.cloned.1.call-done = f32[4,128,128]{2,1,0:T(8,128)} async-done(((f32[4,128,128]{2,1,0:T(8,128)}), f32[4,128,128]{2,1,0:T(8,128)}) %all-reduce.2.cloned.1.call-update) | async-done | bytes 262160 | tf_op jit(solution)/shard_map/psum | solution.py:140
  185.8 4.9 %all_gather.23 = f32[2,128,128]{2,1,0:T(8,128)S(1)} all-gather(f32[1,128,128]{2,1,0:T(8,128)S(1)} %add_multiply_fusion), channel_id=1, replica_groups=mesh['grp'=2,'trade'=4,'date'=2,'path'=2] {'date'}, dimensions={0}, use_global_device_ids=true | all-gather | bytes 196608 | tf_op jit(solution)/shard_map/all_gather | solution.py:13
  (153 shorter events, 63.8 us)
Async XLA Ops:
  7.2 13.6 %copy-start = (f32[4,128,128]{2,1,0:T(8,128)S(1)}, f32[4,128,128]{2,1,0:T(8,128)}, u32[]{:S(2)}) copy-start(f32[4,128,128]{2,1,0:T(8,128)} %param.15) | copy-start | bytes 786436
  7.2 77.3 %reduce-scatter.2.cloned.1.call-start = ((), (), s32[]{:S(2)}) async-start(), calls=%async_computation.1 | async-start | bytes 327680 | tf_op jit(solution)/shard_map/reduce_scatter | solution.py:102
  20.8 41.0 %copy-start.2 = (s32[64]{0:T(128)S(1)}, s32[64]{0:T(128)}, u32[]{:S(2)}) copy-start(s32[64]{0:T(128)} %param.19) | copy-start | bytes 772
  20.9 42.2 %copy-start.3 = (f32[4,32]{1,0:T(4,128)S(1)}, f32[4,32]{1,0:T(4,128)}, u32[]{:S(2)}) copy-start(f32[4,32]{1,0:T(4,128)} %param.21) | copy-start | bytes 1540
  20.9 63.7 %copy-start.4 = (f32[32]{0:T(128)S(1)}, f32[32]{0:T(128)}, u32[]{:S(2)}) copy-start(f32[32]{0:T(128)} %param.20) | copy-start | bytes 388
  63.0 121.9 %all-reduce.2.cloned.1.call-start = ((), (), s32[]{:S(2)}) async-start(), calls=%async_computation.2 | async-start | bytes 524288 | tf_op jit(solution)/shard_map/psum | solution.py:140
  150.0 0.7 copy-start.1
Sparse Core Ops, SparseCore 0:
  63.1 21.3 reduce-scatter.1
  150.9 33.9 all-reduce.1
where the time goes:
time: 202 us; the launch traced here: 200 us
  matrix products  54.4 us (27%)
  waiting for transfers between devices  47.1 us (23%)
  local copies, waits for them, and re-layouts  38.5 us (19%)
  blocking collectives  36.4 us (18%)
  between operations  14.2 us (7%)
  other arithmetic  8.08 us (4%)
    dot_general x16, matrix products, value_group(): jnp.dot(state_bf, sensitivity_portion, preferred_element_type=jnp.float32)  28 us
    psum x1, waiting for transfers between devices, shards(): summed = lax.psum(direct, 'trade')  25.7 us
    dot_general x16, matrix products, pull_group(): lax.dot_general(value_adjoint, sensitivity_portion, (((1,), (1,)), ((), (...  25.1 us
    reduce_scatter x1, waiting for transfers between devices, shards(): lax.psum_scatter(partial_value, 'trade', scatter_dimension=0, tiled=True)  21.4 us
    all_gather x4, blocking collectives, entering(): everything = jax.tree.map(lambda part: lax.all_gather(part, axis), value)  19.2 us
    all_gather x1, blocking collectives, shards(): gathered = lax.all_gather(net_adjoint, 'trade', axis=0, tiled=True)  13.8 us
    dynamic_slice x16, local copies, waits for them, and re-layouts, value_group(): lax.dynamic_slice_in_dim(signed_notional, opening_offset, cluster_extent, 0)  12.2 us
    dynamic_slice x16, local copies, waits for them, and re-layouts, pull_group(): lax.dynamic_slice_in_dim(signed_notional, opening_offset, cluster_extent, 0)  12.2 us
  transfers between devices with their start and end apart: 2, of which 2 were waited for; matrix products, arithmetic and copies ran while one was open for 0% of the time, Pallas kernels for 0%

commit v1 on v0

--- a/solution.py
+++ b/solution.py
@@ -108,7 +108,15 @@
         default_discount_mass.T[:, :, None]
         * jax.nn.sigmoid(shifted).reshape(cpty_dev, date_count, path_count)
     ).reshape(cpty_dev, row_count)
-    gathered = lax.all_gather(net_adjoint, "trade", axis=0, tiled=True)
+    ways, here, step = (lax.axis_size("trade"), lax.axis_index("trade"), net_adjoint.shape[0])
+    line, have = (net_adjoint, 1)
+    while have < ways:
+        line = jnp.concatenate(
+            [line, lax.ppermute(line, "trade", [(d, (d - have) % ways) for d in range(ways)])],
+            axis=0,
+        )
+        have = 2 * have
+    gathered = jnp.roll(line, here * step, axis=0)
     block_adjoint = jnp.dot(ownership, gathered, precision=highest)
 
     def pull_group(group_index, running):

time: 202 us -> 201 us (level)
  blocking collectives: 36.4 us -> 22.6 us
  waiting for transfers between devices: 47.1 us -> 58.1 us
    all_gather x1 -> x0, blocking collectives: 13.8 us -> none  [shards(): gathered = lax.all_gather(net_adjoint, 'trade', axis=0, tiled=True)]
    ppermute x0 -> x2, waiting for transfers between devices: none -> 9.79 us  [shards(): lax.ppermute(line, 'trade', [(d, (d - have) % ways) for d in range(ways)])]
  transfers between devices with their start and end apart: 2 -> 4, of which waited for: 2 -> 4; matrix products, arithmetic and copies ran while one was open for 0% -> 0% of each run, Pallas kernels for 0% -> 0%
where the time goes in v1:
time: 201 us; the launch traced here: 199 us
  waiting for transfers between devices  58.1 us (29%)
  matrix products  54.4 us (27%)
  local copies, waits for them, and re-layouts  38.5 us (19%)
  blocking collectives  22.6 us (11%)
  between operations  14.3 us (7%)
  other arithmetic  8.09 us (4%)
    dot_general x16, matrix products, value_group(): jnp.dot(state_bf, sensitivity_portion, preferred_element_type=jnp.float32)  28 us
    psum x1, waiting for transfers between devices, shards(): summed = lax.psum(direct, 'trade')  26.9 us
    dot_general x16, matrix products, pull_group(): lax.dot_general(value_adjoint, sensitivity_portion, (((1,), (1,)), ((), (...  25.1 us
    reduce_scatter x1, waiting for transfers between devices, shards(): lax.psum_scatter(partial_value, 'trade', scatter_dimension=0, tiled=True)  21.4 us
    all_gather x4, blocking collectives, entering(): everything = jax.tree.map(lambda part: lax.all_gather(part, axis), value)  19.2 us
    dynamic_slice x16, local copies, waits for them, and re-layouts, value_group(): lax.dynamic_slice_in_dim(signed_notional, opening_offset, cluster_extent, 0)  12.2 us
    dynamic_slice x16, local copies, waits for them, and re-layouts, pull_group(): lax.dynamic_slice_in_dim(signed_notional, opening_offset, cluster_extent, 0)  12.2 us
    ppermute x2, waiting for transfers between devices, shards(): lax.ppermute(line, 'trade', [(d, (d - have) % ways) for d in range(ways)])  9.79 us
  transfers between devices with their start and end apart: 4, of which 4 were waited for; matrix products, arithmetic and copies ran while one was open for 0% of the time, Pallas kernels for 0%

profile of v1, /device:TPU:0, one launch (start us, length us, event | category | flops | bytes accessed | tf_op | source)
XLA Modules:
  0.0 198.7 jit_solution(11477016559130328201)
XLA Ops:
  8.8 5.1 %all-gather = f32[2,1,128]{2,1,0:T(1,128)S(1)} all-gather(f32[1,1,128]{2,1,0:T(1,128)S(1)} %get-tuple-element.551), channel_id=1, replica_groups=mesh['grp'=2,'trade'=4,'date'=2,'path'=2] {'date'}, dimensions={0}, use_global_device_ids=true | all-gather | bytes 1536 | tf_op jit(solution)/shard_map/all_gather | solution.py:13
  14.8 4.9 %all_gather.17 = f32[2,128,128]{2,1,0:T(8,128)S(1)} all-gather(f32[1,128,128]{2,1,0:T(8,128)S(1)} %multiply_add_fusion), channel_id=1, replica_groups=mesh['grp'=2,'trade'=4,'date'=2,'path'=2] {'date'}, dimensions={0}, use_global_device_ids=true | all-gather | bytes 196608 | tf_op jit(solution)/shard_map/all_gather | solution.py:13
  20.9 41.0 %while.57 = (s32[]{:T(128)}, f32[64,512]{1,0:T(8,128)S(1)}, bf16[128,8192]{1,0:T(8,128)(2,1)}, bf16[512,128]{1,0:T(8,128)(2,1)S(1)}, f32[8192]{0:T(1024)}, /*ind...) while((s32[]{:T(128)}, f32[64,512]{1,0:T(8,128)S(1)}, ...), condition=%wide.region_4.5_spmd, body=%wide.region_2.4_spmd.sunk | while | flops 69203976 | bytes 293085 | solution.py:91
  21.7 1.8 bitcast_reduce_fusion.2
  24.2 1.8 bitcast_reduce_fusion.2
  26.8 1.8 bitcast_reduce_fusion.2
  29.4 1.8 bitcast_reduce_fusion.2
  31.9 1.8 bitcast_reduce_fusion.2
  34.5 1.8 bitcast_reduce_fusion.2
  37.0 1.8 bitcast_reduce_fusion.2
  39.6 1.7 bitcast_reduce_fusion.2
  42.2 1.8 bitcast_reduce_fusion.2
  44.7 1.8 bitcast_reduce_fusion.2
  47.3 1.8 bitcast_reduce_fusion.2
  49.8 1.7 bitcast_reduce_fusion.2
  52.4 1.8 bitcast_reduce_fusion.2
  55.0 1.8 bitcast_reduce_fusion.2
  57.5 1.8 bitcast_reduce_fusion.2
  60.1 1.8 bitcast_reduce_fusion.2
  63.1 21.4 %reduce-scatter.2.cloned.1.call-done = f32[32,512]{1,0:T(8,128)} async-done(((f32[128,512]{1,0:T(8,128)}), f32[32,512]{1,0:T(8,128)}) %reduce-scatter.2.cloned.1.call-update) | async-done | bytes 65552 | tf_op jit(solution)/shard_map/reduce_scatter | solution.py:102
  86.1 3.8 %collective-permute-done = f32[32,512]{1,0:T(8,128)S(1)} collective-permute-done((f32[32,512]{1,0:T(8,128)S(1)}, f32[32,512]{1,0:T(8,128)S(1)}, u32[]{:S(2)}, u32[]{:S(2)}) %collective-permute-start) | collective-permute-done | bytes 65568 | tf_op jit(solution)/shard_map/ppermute | solution.py:115
  90.6 6.0 %collective-permute-done.1 = f32[64,512]{1,0:T(8,128)S(1)} collective-permute-done((f32[64,512]{1,0:T(8,128)S(1)}, f32[64,512]{1,0:T(8,128)S(1)}, u32[]{:S(2)}, u32[]{:S(2)}) %collective-permute-start.1) | collective-permute-done | bytes 131104 | tf_op jit(solution)/shard_map/ppermute | solution.py:115
  96.9 50.3 %while.59 = (s32[]{:T(128)}, f32[512,128]{1,0:T(8,128)S(1)}, f32[64,512]{1,0:T(8,128)S(1)}, bf16[128,8192]{1,0:T(8,128)(2,1)}, bf16[512,128]{1,0:T(8,128)(2,1)S(...) while((s32[]{:T(128)}, f32[512,128]{1,0:T(8,128)S(1)}, ...), condition=%wide.region_9.10_spmd.clone, body=%wide.region_8.9_spmd.clone.sunk | while | flops 135921680 | bytes 3063530 | solution.py:144
  98.5 1.6 fusion.51
  101.7 1.6 fusion.51
  111.1 1.6 fusion.51
  129.9 1.6 fusion.51
  142.5 1.6 fusion.51
  148.0 4.2 %all-gather.1 = f32[2,1,128]{2,1,0:T(1,128)S(1)} all-gather(f32[1,1,128]{2,1,0:T(1,128)S(1)} %get-tuple-element.547), channel_id=1, replica_groups=mesh['grp'=2,'trade'=4,'date'=2,'path'=2] {'date'}, dimensions={0}, use_global_device_ids=true | all-gather | bytes 1536 | tf_op jit(solution)/shard_map/all_gather | solution.py:13
  152.4 3.4 %psum.14 = f32[4,32]{0,1:T(8,128)S(1)} all-reduce(f32[4,32]{0,1:T(8,128)S(1)} %bitcast.153), channel_id=1, replica_groups=mesh['grp'=2,'trade'=4,'date'=2,'path'=2] {'path'}, use_global_device_ids=true, to_apply=%region_7.8 | all-reduce | flops 128 | bytes 1024 | tf_op jit(solution)/shard_map/psum | solution.py:105
  156.4 26.9 %all-reduce.2.cloned.1.call-done = f32[4,128,128]{2,1,0:T(8,128)} async-done(((f32[4,128,128]{2,1,0:T(8,128)}), f32[4,128,128]{2,1,0:T(8,128)}) %all-reduce.2.cloned.1.call-update) | async-done | bytes 262160 | tf_op jit(solution)/shard_map/psum | solution.py:148
  184.3 4.9 %all_gather.19 = f32[2,128,128]{2,1,0:T(8,128)S(1)} all-gather(f32[1,128,128]{2,1,0:T(8,128)S(1)} %add_multiply_fusion), channel_id=1, replica_groups=mesh['grp'=2,'trade'=4,'date'=2,'path'=2] {'date'}, dimensions={0}, use_global_device_ids=true | all-gather | bytes 196608 | tf_op jit(solution)/shard_map/all_gather | solution.py:13
  (162 shorter events, 66.7 us)
Async XLA Ops:
  7.2 13.6 %copy-start = (f32[4,128,128]{2,1,0:T(8,128)S(1)}, f32[4,128,128]{2,1,0:T(8,128)}, u32[]{:S(2)}) copy-start(f32[4,128,128]{2,1,0:T(8,128)} %param.15) | copy-start | bytes 786436
  7.2 77.3 %reduce-scatter.2.cloned.1.call-start = ((), (), s32[]{:S(2)}) async-start(), calls=%async_computation.1 | async-start | bytes 327680 | tf_op jit(solution)/shard_map/reduce_scatter | solution.py:102
  20.8 41.0 %copy-start.2 = (s32[64]{0:T(128)S(1)}, s32[64]{0:T(128)}, u32[]{:S(2)}) copy-start(s32[64]{0:T(128)} %param.19) | copy-start | bytes 772
  20.9 42.2 %copy-start.3 = (f32[4,32]{1,0:T(4,128)S(1)}, f32[4,32]{1,0:T(4,128)}, u32[]{:S(2)}) copy-start(f32[4,32]{1,0:T(4,128)} %param.21) | copy-start | bytes 1540
  20.9 63.7 %copy-start.4 = (f32[32]{0:T(128)S(1)}, f32[32]{0:T(128)}, u32[]{:S(2)}) copy-start(f32[32]{0:T(128)} %param.20) | copy-start | bytes 388
  63.0 120.3 %all-reduce.2.cloned.1.call-start = ((), (), s32[]{:S(2)}) async-start(), calls=%async_computation.2 | async-start | bytes 524288 | tf_op jit(solution)/shard_map/psum | solution.py:148
  85.6 4.3 %collective-permute-start = (f32[32,512]{1,0:T(8,128)S(1)}, f32[32,512]{1,0:T(8,128)S(1)}, u32[]{:S(2)}, u32[]{:S(2)}) collective-permute-start(f32[32,512]{1,0:T(8,128)S(1)} %get-tuple-element.539), channel_id=1, source_target_pairs={{0,12},{4,0},{8,4},{12,8},{1,13},{5,1},{9,5},{13,9},{2,14},{6,2},{... | collective-permute-start | bytes 196616 | tf_op jit(solution)/shard_map/ppermute | solution.py:115
  89.9 6.7 %collective-permute-start.1 = (f32[64,512]{1,0:T(8,128)S(1)}, f32[64,512]{1,0:T(8,128)S(1)}, u32[]{:S(2)}, u32[]{:S(2)}) collective-permute-start(f32[64,512]{1,0:T(8,128)S(1)} %pad_maximum_fusion.2), channel_id=1, source_target_pairs={{0,8},{4,12},{8,0},{12,4},{1,9},{5,13},{9,1},{13,5},{2,10},{6,14},... | collective-permute-start | bytes 393224 | tf_op jit(solution)/shard_map/ppermute | solution.py:115
  147.3 0.7 copy-start.1
Sparse Core Ops, SparseCore 0:
  63.1 21.3 reduce-scatter.1
  148.1 35.1 all-reduce.1
